TPU v7x, 32 devices: a whole 2x2x4 slice. The times are simulated.
32 devices in a mesh: rep: 2 (over y), cache: 8 (over z, x), head: 2 (over core).
Axes of the slice: x: 2, y: 2, z: 4, core: 2. Of those that a mesh axis runs over, the one named last changes fastest.
Arguments:
- reception_vectors: bfloat16 [16, 128, 4096], P(('rep', 'cache'), None, 'head'), parts along dimension 0, may hold values from -6 to 6
- address_vectors: bfloat16 [16, 128, 4096], P(('rep', 'cache'), None, 'head'), parts along dimension 0, may hold values from -0.75 to 0.75
- payload_vectors: bfloat16 [16, 128, 4096], P(('rep', 'cache'), None, 'head'), parts along dimension 0, may hold values from -6 to 6
- emission_switch_preact: bfloat16 [16, 128, 4096], P(('rep', 'cache'), None, 'head'), parts along dimension 0, may hold values from -6 to 6
- fading_rates: bfloat16 [16, 128, 4096], P(('rep', 'cache'), None, 'head'), parts along dimension 0, may hold values from 0 to 1, as said below
- present_extra_coefficient: float32 [64, 64], P('head'), may hold values from -5 to 5
- saved_memory_matrix: bfloat16 [64, 64, 64, 64], P(('rep', 'cache'), 'head'), parts along dimension 0, may hold values from -6 to 6
- layernorm_scale: float32 [4096], P('head'), may hold values from 0.1 to 1.9
- layernorm_shift: float32 [4096], P('head'), may hold values from -3 to 3
- stored_memory_locator: int32 [16, 2], P(('rep', 'cache')), parts along dimension 0, may hold values from 0 to 7, as said below
Outputs:
- mixed: bfloat16 [16, 128, 4096], P(('rep', 'cache'), None, 'head'), parts along dimension 0
- final_states: float32 [16, 64, 64, 64], P(('rep', 'cache'), 'head'), parts along dimension 0
There are 2 independent parts, one for each index of `rep`. A program takes and returns all parts, laid end to end along the dimension named above; an argument that names none is the same for every part. Nothing has to cross between parts.
Inputs may be any that keep to these rules, and one draw needn't show every extreme that they name: `fading_rates`: positive decay rates. `stored_memory_locator`: the requests that name one cache index name at most 2 distinct slots of it, and in every draw some cache index has exactly 2 named slots.
All inputs are finite; a program needn't handle non-finite values.
Results may differ from a plain program's by a relative error of at most 0.001.
Values may be sent and summed in bfloat16 or wider, within the bound.
No kernel may reach another device: no remote copies, remote signals or barrier semaphores. Data moves between devices by JAX's collectives and lax.ppermute only.
A program may use at most 64 MiB of HBM per device.

v0:
```python
import jax
import jax.numpy as jnp
from jax import lax
from jax.sharding import PartitionSpec as P

GROUP = 64
HITS = 2


def linear_attention_scan(
    reception_vectors,
    address_vectors,
    payload_vectors,
    fading_rates,
    present_extra_coefficient,
    initial_memory,
):
    length, head_count, group_features = reception_vectors.shape
    blocks = length // GROUP

    def arrange(values):
        return values.reshape(blocks, GROUP, head_count, group_features).transpose(0, 2, 1, 3)

    positions = jnp.arange(GROUP)
    strict_lower = positions[:, None] > positions[None, :]
    identity = jnp.eye(GROUP, dtype=jnp.float32)
    highest = lax.Precision.HIGHEST

    def advance(carry_state, block_data):
        reception_portion, address_portion, value_part, forget_part = block_data
        decay_sum = jnp.cumsum(-forget_part, axis=1)
        before = decay_sum + forget_part
        queries = reception_portion * jnp.exp(before)
        scaled_keys = address_portion * jnp.exp(-decay_sum)
        scores = jnp.einsum("htc,hjc->htj", queries, scaled_keys, precision=highest)
        diagonal_term = jnp.sum(
            reception_portion * present_extra_coefficient[:, None, :] * address_portion, axis=2
        )
        scores = (
            jnp.where(strict_lower[None], scores, 0.0) + diagonal_term[:, :, None] * identity[None]
        )
        emitted_entries = jnp.einsum("htj,hjv->htv", scores, value_part, precision=highest)
        emitted_entries = emitted_entries + jnp.einsum(
            "htc,hcv->htv", queries, carry_state, precision=highest
        )
        group_total = decay_sum[:, -1:, :]
        carried = address_portion * jnp.exp(group_total - decay_sum)
        carry_state = jnp.exp(group_total[:, 0, :])[:, :, None] * carry_state + jnp.einsum(
            "hjc,hjv->hcv", carried, value_part, precision=highest
        )
        return (carry_state, emitted_entries)

    terminal_memory, emitted_entries = lax.scan(
        advance,
        initial_memory,
        (
            arrange(reception_vectors),
            arrange(address_vectors),
            arrange(payload_vectors),
            arrange(fading_rates),
        ),
    )
    emitted_entries = emitted_entries.transpose(0, 2, 1, 3).reshape(
        length, head_count, group_features
    )
    return (emitted_entries, terminal_memory)


def finish(emitted_entries, emission_switch_preact, layernorm_scale, layernorm_shift):
    head_mean = jnp.mean(emitted_entries, axis=2, keepdims=True)
    centered = emitted_entries - head_mean
    head_var = jnp.mean(centered * centered, axis=2, keepdims=True)
    normed = (centered * lax.rsqrt(head_var + 1e-05)).reshape(emitted_entries.shape[0], -1)
    gate_float = emission_switch_preact.astype(jnp.float32)
    return ((normed * layernorm_scale + layernorm_shift) * jax.nn.silu(gate_float)).astype(
        jnp.bfloat16
    )


def body(
    reception_vectors,
    address_vectors,
    payload_vectors,
    emission_switch_preact,
    fading_rates,
    present_extra_coefficient,
    saved_memory_matrix,
    layernorm_scale,
    layernorm_shift,
    stored_memory_locator,
):
    devices = lax.axis_size("cache")
    own_index = lax.axis_index("cache")
    device_groups, group_features = present_extra_coefficient.shape
    slot_count = saved_memory_matrix.shape[0]
    piece_len = device_groups * group_features * group_features // devices
    hit_table = lax.all_gather(stored_memory_locator, "cache", axis=0, tiled=True)
    request_owner = hit_table[:, 0]
    request_slot = hit_table[:, 1]
    owner_ids = jnp.arange(devices, dtype=jnp.int32)
    slot_ids = jnp.arange(slot_count, dtype=jnp.int32)
    owner_match = (request_owner[:, None] == owner_ids[None, :]).astype(jnp.int32)
    slot_match = (request_slot[:, None] == slot_ids[None, :]).astype(jnp.int32)
    counts = jnp.dot(owner_match.T, slot_match, preferred_element_type=jnp.int32)
    used_slots = (counts > 0).astype(jnp.int32)
    slot_rank = jnp.cumsum(used_slots, axis=1) - used_slots
    is_mine = (owner_ids == own_index)[:, None]
    used_mine = jnp.sum(jnp.where(is_mine, used_slots, 0), axis=0)
    rank_mine = jnp.sum(jnp.where(is_mine, slot_rank, 0), axis=0)
    hit_ids = jnp.arange(HITS, dtype=jnp.int32)
    selector = ((rank_mine[None, :] == hit_ids[:, None]) & (used_mine[None, :] > 0)).astype(
        jnp.bfloat16
    )
    flat_cache = saved_memory_matrix.reshape(slot_count, -1)
    compact = jnp.dot(selector, flat_cache, preferred_element_type=jnp.float32).astype(jnp.bfloat16)
    outgoing = compact.reshape(1, HITS, devices, piece_len)
    arrived = lax.all_to_all(outgoing, "cache", split_axis=2, concat_axis=0, tiled=True)
    arrived = arrived.reshape(devices * HITS, piece_len)
    request_rank = jnp.sum(
        jnp.dot(owner_match, slot_rank, preferred_element_type=jnp.int32) * slot_match, axis=1
    )
    wanted = request_owner * HITS + request_rank
    selected = jnp.take(arrived, wanted, axis=0)
    delivered = lax.all_to_all(selected, "cache", split_axis=0, concat_axis=0, tiled=True)
    initial_memory = delivered.reshape(device_groups, group_features, group_features).astype(
        jnp.float32
    )
    head_shape = (reception_vectors.shape[1], device_groups, group_features)

    def divide_among_groups(values):
        return values[0].astype(jnp.float32).reshape(head_shape)

    emitted_entries, terminal_memory = linear_attention_scan(
        divide_among_groups(reception_vectors),
        divide_among_groups(address_vectors),
        divide_among_groups(payload_vectors),
        divide_among_groups(fading_rates),
        present_extra_coefficient,
        initial_memory,
    )
    mixed = finish(emitted_entries, emission_switch_preact[0], layernorm_scale, layernorm_shift)
    return (mixed[None], terminal_memory[None])


def solution(mesh):
    in_specs = (
        P(("rep", "cache"), None, "head"),
        P(("rep", "cache"), None, "head"),
        P(("rep", "cache"), None, "head"),
        P(("rep", "cache"), None, "head"),
        P(("rep", "cache"), None, "head"),
        P("head", None),
        P(("rep", "cache"), "head", None, None),
        P("head"),
        P("head"),
        P(("rep", "cache"), None),
    )
    out_specs = (P(("rep", "cache"), None, "head"), P(("rep", "cache"), "head", None, None))
    return jax.shard_map(body, mesh=mesh, in_specs=in_specs, out_specs=out_specs, check_vma=False)
```

profile of v0, /device:TPU:0, one launch (start us, length us, event | category | flops | bytes accessed | tf_op | source)
XLA Modules:
  0.0 107.3 jit_solution(10807047504298372094)
XLA Ops:
  0.6 22.4 %all-gather = s32[8,1,2]{2,1,0:T(1,128)S(1)} all-gather(s32[1,1,2]{2,1,0:T(1,128)} %bitcast.115), channel_id=1, replica_groups=mesh['rep'=2,'cache'=8,'head'=2] {'cache'}, dimensions={0}, use_global_device_ids=true | all-gather | bytes 72 | tf_op jit(solution)/shard_map/all_gather | solution.py:97
  23.6 2.9 %reshape.200 = bf16[4,131072]{1,0:T(4,128)(2,1)S(1)} reshape(bf16[4,32,64,64]{3,2,1,0:T(8,128)(2,1)} %param.18) | data formatting | bytes 2097152 | tf_op jit(solution)/shard_map/reshape | solution.py:114
  26.5 1.5 %convolution_convert_fusion = bf16[2,131072]{1,0:T(2,128)(2,1)} fusion(bf16[4,131072]{1,0:T(4,128)(2,1)S(1)} %reshape.200, pred[4]{0:T(512)(128)(4,1)S(1)} %broadcast_compare_fusion, s32[4]{0:T(128)S(1)} %get-tuple-element.96), kind=kOutput, calls=%fused_computation.33 | convolution fusion | flops 2359312 | bytes 1572884 | tf_op jit(solution)/shard_map/dot_general | solution.py:115
  28.0 3.5 %all-to-all-start = ((bf16[1,2,8,16384]{3,1,0,2:T(2,128)(2,1)}), bf16[1,2,8,16384]{3,1,0,2:T(2,128)(2,1)S(1)}, u32[]{:S(2)}, u32[]{:S(2)}) async-start(bf16[1,2,8,16384]{3,1,0,2:T(2,128)(2,1)} %bitcast.6), calls=%async_computation | async-start | bytes 1048576 | tf_op jit(solution)/shard_map/all_to_all | solution.py:117
  31.7 10.7 %all-to-all-done = bf16[1,2,8,16384]{3,1,0,2:T(2,128)(2,1)S(1)} async-done(((bf16[1,2,8,16384]{3,1,0,2:T(2,128)(2,1)}), bf16[1,2,8,16384]{3,1,0,2:T(2,128)(2,1)S(1)}, u32[]{:S(2)}, u32[]{:S(2)}) %all-to-all-start) | async-done | bytes 524320 | tf_op jit(solution)/shard_map/all_to_all | solution.py:117
  45.7 3.8 %all-to-all-start.1 = ((bf16[8,2,8192]{2,1,0:T(2,128)(2,1)}), bf16[8,2,8192]{2,1,0:T(2,128)(2,1)S(1)}, u32[]{:S(2)}, u32[]{:S(2)}) async-start(bf16[8,2,8192]{2,1,0:T(2,128)(2,1)} %reshape.220), calls=%async_computation.1 | async-start | bytes 524288 | tf_op jit(solution)/shard_map/all_to_all | solution.py:124
  50.5 2.3 %reshape.208 = f32[2,64,32,64]{3,2,1,0:T(8,128)} reshape(bf16[1,128,2048]{2,1,0:T(8,128)(2,1)S(1)} %copy-done.8) | data formatting | bytes 1572864 | tf_op jit(solution)/shard_map/transpose | solution.py:22
  52.8 2.2 %reshape.206 = f32[2,64,32,64]{3,2,1,0:T(8,128)} reshape(bf16[1,128,2048]{2,1,0:T(8,128)(2,1)S(1)} %copy-done.9) | data formatting | bytes 1572864 | tf_op jit(solution)/shard_map/transpose | solution.py:22
  55.0 2.3 %reshape.207 = f32[2,64,32,64]{3,2,1,0:T(8,128)} reshape(bf16[1,128,2048]{2,1,0:T(8,128)(2,1)S(1)} %copy-done.10) | data formatting | bytes 1572864 | tf_op jit(solution)/shard_map/transpose | solution.py:22
  57.3 2.3 %reshape.205 = f32[2,64,32,64]{3,2,1,0:T(8,128)} reshape(bf16[1,128,2048]{2,1,0:T(8,128)(2,1)S(1)} %copy-done.11) | data formatting | bytes 1572864 | tf_op jit(solution)/shard_map/transpose | solution.py:22
  61.8 34.4 %while.13 = (s32[]{:T(128)}, f32[32,64,64]{2,1,0:T(8,128)S(1)}, f32[2,32,64,64]{3,2,1,0:T(8,128)}, f32[2,32,64,64]{3,1,2,0:T(8,128)}, f32[2,32,64,64]{3,1,2,0:T(...) while((s32[]{:T(128)}, f32[32,64,64]{2,1,0:T(8,128)S(1)}, ...), condition=%wide.region_7.8_spmd.clone, body=%wide.region_4.7_spmd.clone.sunk | while | flops 413018112 | bytes 34734336 | solution.py:53
  64.5 3.4 %bitcast_multiply_fusion.6 = (f32[32,64,64]{2,0,1:T(8,128)}, f32[32,64,64]{2,0,1:T(8,128)}, f32[32,64]{0,1:T(8,128)S(1)}, f32[32,64,64]{2,0,1:T(8,128)S(1)}) fusion(f32[32,64,64]{2,0,1:T(8,128)S(1)} %fusion.58, f32[2,32,64,64]{3,1,2,0:T(8,128)} %get-tuple-element.207, s32[]{:T(128)S(6)} %copy.71, f32[32,64]{1,0:T(8,128)S(1)} %slice_bitcast_fusion.4, ...), kind=kLoop, calls=%fused_computation.14.clone.1 | loop fusion | flops 1177600 | bytes 3694596 | tf_op jit(solution)/shard_map/while/body/eval_jaxpr/mul | solution.py:34
  68.0 4.2 %fusion.60 = f32[32,64,64]{2,1,0:T(8,128)S(1)} fusion(f32[32,64,64]{2,0,1:T(8,128)} %get-tuple-element.180, f32[32,64,64]{2,0,1:T(8,128)S(1)} %get-tuple-element.181, f32[64,64]{1,0:T(8,128)S(1)} %get-tuple-element.182, f32[32,64]{1,0:T(8,128)S(1)} %copy.66, pred[64,64]{1,0:T(8,128)(4,1)S(1)} %get-tuple-element.184), kind=kOutput, calls=%fused_computation.8.clone.1 | convolution fusion | flops 101056512 | bytes 1601536 | tf_op jit(solution)/shard_map/while/body/eval_jaxpr/htc,hjc->htj/dot_general | solution.py:35
  72.2 1.8 %fusion.61 = f32[32,64,64]{2,1,0:T(8,128)S(1)} fusion(f32[32,64,64]{2,1,0:T(8,128)S(1)} %fusion.60, f32[1,32,64,64]{3,1,2,0:T(8,128)S(1)} %constant_dynamic-slice_fusion.2), kind=kOutput, calls=%fused_computation.22.clone.1 | convolution fusion | flops 100663296 | bytes 1572864 | tf_op jit(solution)/shard_map/while/body/eval_jaxpr/htj,hjv->htv/dot_general | solution.py:42
  74.0 1.8 %fusion.62 = f32[2,32,64,64]{3,2,1,0:T(8,128)S(1)} fusion(f32[2,32,64,64]{3,2,1,0:T(8,128)S(1)} %copy-done.4, s32[]{:T(128)S(6)} %copy.71, f32[32,64,64]{2,1,0:T(8,128)S(1)} %fusion.61, f32[32,64,64]{2,1,0:T(8,128)S(1)} %get-tuple-element.195, f32[32,64,64]{2,0,1:T(8,128)S(1)} %get-tuple-element.181), kind=kOutput, calls=%fused_computation.5.clone.1 | convolution fusion | flops 100794368 | bytes 4194308 | tf_op jit(solution)/shard_map/while/body/eval_jaxpr/htc,hcv->htv/dot_general | solution.py:43
  75.8 3.2 %convolution_add_fusion.3 = f32[32,64,64]{2,1,0:T(8,128)S(1)} fusion(f32[32,64,64]{2,0,1:T(8,128)S(1)} %copy-done.1, f32[32,64,64]{2,1,0:T(8,128)S(1)} %get-tuple-element.195, f32[1,32,64,64]{3,1,2,0:T(8,128)S(1)} %constant_dynamic-slice_fusion.2, f32[32,64]{1,0:T(8,128)S(1)} %fusion.59), kind=kOutput, calls=%fused_computation.6.clone.1 | convolution fusion | flops 100925440 | bytes 2105344 | tf_op jit(solution)/shard_map/while/body/eval_jaxpr/hjc,hjv->hcv/dot_general | solution.py:48
  81.6 3.4 %bitcast_multiply_fusion.6 = (f32[32,64,64]{2,0,1:T(8,128)}, f32[32,64,64]{2,0,1:T(8,128)}, f32[32,64]{0,1:T(8,128)S(1)}, f32[32,64,64]{2,0,1:T(8,128)S(1)}) fusion(f32[32,64,64]{2,0,1:T(8,128)S(1)} %fusion.58, f32[2,32,64,64]{3,1,2,0:T(8,128)} %get-tuple-element.207, s32[]{:T(128)S(6)} %copy.71, f32[32,64]{1,0:T(8,128)S(1)} %slice_bitcast_fusion.4, ...), kind=kLoop, calls=%fused_computation.14.clone.1 | loop fusion | flops 1177600 | bytes 3694596 | tf_op jit(solution)/shard_map/while/body/eval_jaxpr/mul | solution.py:34
  85.1 4.2 %fusion.60 = f32[32,64,64]{2,1,0:T(8,128)S(1)} fusion(f32[32,64,64]{2,0,1:T(8,128)} %get-tuple-element.180, f32[32,64,64]{2,0,1:T(8,128)S(1)} %get-tuple-element.181, f32[64,64]{1,0:T(8,128)S(1)} %get-tuple-element.182, f32[32,64]{1,0:T(8,128)S(1)} %copy.66, pred[64,64]{1,0:T(8,128)(4,1)S(1)} %get-tuple-element.184), kind=kOutput, calls=%fused_computation.8.clone.1 | convolution fusion | flops 101056512 | bytes 1601536 | tf_op jit(solution)/shard_map/while/body/eval_jaxpr/htc,hjc->htj/dot_general | solution.py:35
  89.4 1.8 %fusion.61 = f32[32,64,64]{2,1,0:T(8,128)S(1)} fusion(f32[32,64,64]{2,1,0:T(8,128)S(1)} %fusion.60, f32[1,32,64,64]{3,1,2,0:T(8,128)S(1)} %constant_dynamic-slice_fusion.2), kind=kOutput, calls=%fused_computation.22.clone.1 | convolution fusion | flops 100663296 | bytes 1572864 | tf_op jit(solution)/shard_map/while/body/eval_jaxpr/htj,hjv->htv/dot_general | solution.py:42
  91.1 1.8 %fusion.62 = f32[2,32,64,64]{3,2,1,0:T(8,128)S(1)} fusion(f32[2,32,64,64]{3,2,1,0:T(8,128)S(1)} %copy-done.4, s32[]{:T(128)S(6)} %copy.71, f32[32,64,64]{2,1,0:T(8,128)S(1)} %fusion.61, f32[32,64,64]{2,1,0:T(8,128)S(1)} %get-tuple-element.195, f32[32,64,64]{2,0,1:T(8,128)S(1)} %get-tuple-element.181), kind=kOutput, calls=%fused_computation.5.clone.1 | convolution fusion | flops 100794368 | bytes 4194308 | tf_op jit(solution)/shard_map/while/body/eval_jaxpr/htc,hcv->htv/dot_general | solution.py:43
  92.9 3.2 %convolution_add_fusion.3 = f32[32,64,64]{2,1,0:T(8,128)S(1)} fusion(f32[32,64,64]{2,0,1:T(8,128)S(1)} %copy-done.1, f32[32,64,64]{2,1,0:T(8,128)S(1)} %get-tuple-element.195, f32[1,32,64,64]{3,1,2,0:T(8,128)S(1)} %constant_dynamic-slice_fusion.2, f32[32,64]{1,0:T(8,128)S(1)} %fusion.59), kind=kOutput, calls=%fused_computation.6.clone.1 | convolution fusion | flops 100925440 | bytes 2105344 | tf_op jit(solution)/shard_map/while/body/eval_jaxpr/hjc,hjv->hcv/dot_general | solution.py:48
  96.2 2.6 %bitcast_reduce_fusion = f32[2,64,32]{1,2,0:T(8,128)S(1)} fusion(f32[2,32,64,64]{3,2,1,0:T(8,128)} %get-tuple-element.55), kind=kLoop, calls=%fused_computation.75 | loop fusion | flops 258048 | bytes 1064960 | tf_op jit(solution)/shard_map/reduce_sum | solution.py:70
  100.5 2.4 %copy.35 = f32[2,64,32,64]{1,0,3,2:T(2,128)} copy(f32[2,64,32,64]{3,1,2,0:T(8,128)S(1)} %bitcast.110) | data formatting | bytes 2097152 | tf_op jit(solution)/shard_map/transpose | solution.py:63
  102.8 2.6 %reshape.203 = f32[1,128,2048]{1,2,0:T(8,128)S(1)} reshape(f32[2,64,32,64]{1,0,3,2:T(2,128)} %copy.35) | data formatting | bytes 2097152 | tf_op jit(solution)/shard_map/reshape | solution.py:63
  (85 shorter events, 15.5 us)
Async XLA Ops:
  28.0 14.4 %all-to-all-start = ((bf16[1,2,8,16384]{3,1,0,2:T(2,128)(2,1)}), bf16[1,2,8,16384]{3,1,0,2:T(2,128)(2,1)S(1)}, u32[]{:S(2)}, u32[]{:S(2)}) async-start(bf16[1,2,8,16384]{3,1,0,2:T(2,128)(2,1)} %bitcast.6), calls=%async_computation | async-start | bytes 1048576 | tf_op jit(solution)/shard_map/all_to_all | solution.py:117
  42.6 6.9 %copy-start.12 = (bf16[1,128,2048]{2,1,0:T(8,128)(2,1)S(1)}, bf16[1,128,2048]{2,1,0:T(8,128)(2,1)}, u32[]{:S(2)}) copy-start(bf16[1,128,2048]{2,1,0:T(8,128)(2,1)} %param.15) | copy-start | bytes 1572868
  43.4 7.2 %copy-start.8 = (bf16[1,128,2048]{2,1,0:T(8,128)(2,1)S(1)}, bf16[1,128,2048]{2,1,0:T(8,128)(2,1)}, u32[]{:S(2)}) copy-start(bf16[1,128,2048]{2,1,0:T(8,128)(2,1)} %param.12) | copy-start | bytes 1572868
  45.7 7.1 %copy-start.9 = (bf16[1,128,2048]{2,1,0:T(8,128)(2,1)S(1)}, bf16[1,128,2048]{2,1,0:T(8,128)(2,1)}, u32[]{:S(2)}) copy-start(bf16[1,128,2048]{2,1,0:T(8,128)(2,1)} %param.13) | copy-start | bytes 1572868
  45.7 13.9 %all-to-all-start.1 = ((bf16[8,2,8192]{2,1,0:T(2,128)(2,1)}), bf16[8,2,8192]{2,1,0:T(2,128)(2,1)S(1)}, u32[]{:S(2)}, u32[]{:S(2)}) async-start(bf16[8,2,8192]{2,1,0:T(2,128)(2,1)} %reshape.220), calls=%async_computation.1 | async-start | bytes 524288 | tf_op jit(solution)/shard_map/all_to_all | solution.py:124
  50.5 4.5 %copy-start.10 = (bf16[1,128,2048]{2,1,0:T(8,128)(2,1)S(1)}, bf16[1,128,2048]{2,1,0:T(8,128)(2,1)}, u32[]{:S(2)}) copy-start(bf16[1,128,2048]{2,1,0:T(8,128)(2,1)} %param.14) | copy-start | bytes 1572868
  52.8 4.5 %copy-start.11 = (bf16[1,128,2048]{2,1,0:T(8,128)(2,1)S(1)}, bf16[1,128,2048]{2,1,0:T(8,128)(2,1)}, u32[]{:S(2)}) copy-start(bf16[1,128,2048]{2,1,0:T(8,128)(2,1)} %param.16) | copy-start | bytes 1572868
  59.6 2.2 %copy-start.13 = (f32[32,64]{1,0:T(8,128)S(1)}, f32[32,64]{1,0:T(8,128)}, u32[]{:S(2)}) copy-start(f32[32,64]{1,0:T(8,128)} %param.17) | copy-start | bytes 24580
  62.0 1.9 %copy-start.2 = (f32[2,32,64,64]{3,1,2,0:T(8,128)S(1)}, f32[2,32,64,64]{3,1,2,0:T(8,128)}, u32[]{:S(2)}) copy-start(f32[2,32,64,64]{3,1,2,0:T(8,128)} %get-tuple-element.208) | copy-start | bytes 3145732 | tf_op jit(solution)/shard_map/while
  62.0 2.5 %copy-start.3 = (f32[2,32,64,64]{3,1,2,0:T(8,128)S(1)}, f32[2,32,64,64]{3,1,2,0:T(8,128)}, u32[]{:S(2)}) copy-start(f32[2,32,64,64]{3,1,2,0:T(8,128)} %get-tuple-element.209) | copy-start | bytes 3145732 | tf_op jit(solution)/shard_map/while
  72.2 1.8 %copy-start.4 = (f32[2,32,64,64]{3,2,1,0:T(8,128)S(1)}, f32[2,32,64,64]{3,2,1,0:T(8,128)}, u32[]{:S(2)}) copy-start(f32[2,32,64,64]{3,2,1,0:T(8,128)} %get-tuple-element.196) | copy-start | bytes 3145732 | tf_op jit(solution)/shard_map/while
  74.0 1.8 %copy-start.1 = (f32[32,64,64]{2,0,1:T(8,128)S(1)}, f32[32,64,64]{2,0,1:T(8,128)}, u32[]{:S(2)}) copy-start(f32[32,64,64]{2,0,1:T(8,128)} %get-tuple-element.179) | copy-start | bytes 1572868 | tf_op jit(solution)/shard_map/while
  75.8 3.3 %copy-start.5 = (f32[2,32,64,64]{3,2,1,0:T(8,128)}, f32[2,32,64,64]{3,2,1,0:T(8,128)S(1)}, u32[]{:S(2)}) copy-start(f32[2,32,64,64]{3,2,1,0:T(8,128)S(1)} %fusion.62) | copy-start | bytes 3145732 | tf_op jit(solution)/shard_map/while
  79.1 1.9 %copy-start.2 = (f32[2,32,64,64]{3,1,2,0:T(8,128)S(1)}, f32[2,32,64,64]{3,1,2,0:T(8,128)}, u32[]{:S(2)}) copy-start(f32[2,32,64,64]{3,1,2,0:T(8,128)} %get-tuple-element.208) | copy-start | bytes 3145732 | tf_op jit(solution)/shard_map/while
  79.1 2.5 %copy-start.3 = (f32[2,32,64,64]{3,1,2,0:T(8,128)S(1)}, f32[2,32,64,64]{3,1,2,0:T(8,128)}, u32[]{:S(2)}) copy-start(f32[2,32,64,64]{3,1,2,0:T(8,128)} %get-tuple-element.209) | copy-start | bytes 3145732 | tf_op jit(solution)/shard_map/while
  89.4 1.8 %copy-start.4 = (f32[2,32,64,64]{3,2,1,0:T(8,128)S(1)}, f32[2,32,64,64]{3,2,1,0:T(8,128)}, u32[]{:S(2)}) copy-start(f32[2,32,64,64]{3,2,1,0:T(8,128)} %get-tuple-element.196) | copy-start | bytes 3145732 | tf_op jit(solution)/shard_map/while
  91.1 1.8 %copy-start.1 = (f32[32,64,64]{2,0,1:T(8,128)S(1)}, f32[32,64,64]{2,0,1:T(8,128)}, u32[]{:S(2)}) copy-start(f32[32,64,64]{2,0,1:T(8,128)} %get-tuple-element.179) | copy-start | bytes 1572868 | tf_op jit(solution)/shard_map/while
  92.9 3.3 %copy-start.5 = (f32[2,32,64,64]{3,2,1,0:T(8,128)}, f32[2,32,64,64]{3,2,1,0:T(8,128)S(1)}, u32[]{:S(2)}) copy-start(f32[2,32,64,64]{3,2,1,0:T(8,128)S(1)} %fusion.62) | copy-start | bytes 3145732 | tf_op jit(solution)/shard_map/while
  96.2 4.0 %copy-start = (f32[32,64,64]{2,1,0:T(8,128)}, f32[32,64,64]{2,1,0:T(8,128)S(1)}, u32[]{:S(2)}) copy-start(f32[32,64,64]{2,1,0:T(8,128)S(1)} %get-tuple-element.56) | copy-start | bytes 1572868
  96.2 2.6 %copy-start.6 = (f32[2,32,64,64]{3,2,1,0:T(8,128)S(1)}, f32[2,32,64,64]{3,2,1,0:T(8,128)}, u32[]{:S(2)}) copy-start(f32[2,32,64,64]{3,2,1,0:T(8,128)} %get-tuple-element.55) | copy-start | bytes 3145732
  102.8 2.7 %copy-start.7 = (bf16[1,128,2048]{1,2,0:T(8,128)(2,1)S(1)}, bf16[1,128,2048]{1,2,0:T(8,128)(2,1)}, u32[]{:S(2)}) copy-start(bf16[1,128,2048]{1,2,0:T(8,128)(2,1)} %copy.38) | copy-start | bytes 1572868
  102.8 2.7 %copy-start.14 = (f32[2048]{0:T(1024)S(1)}, f32[2048]{0:T(1024)}, u32[]{:S(2)}) copy-start(f32[2048]{0:T(1024)} %param.20) | copy-start | bytes 24580
  102.8 2.7 %copy-start.15 = (f32[2048]{0:T(1024)S(1)}, f32[2048]{0:T(1024)}, u32[]{:S(2)}) copy-start(f32[2048]{0:T(1024)} %param.19) | copy-start | bytes 24580
where the time goes:
time: 108 us; the launch traced here: 107 us
  local copies, waits for them, and re-layouts  24.6 us (23%)
  matrix products  23.9 us (22%)
  blocking collectives  22.4 us (21%)
  other arithmetic  17.1 us (16%)
  waiting for transfers between devices  10.7 us (10%)
  starting transfers between devices  7.32 us (7%)
    all_gather x1, blocking collectives, body(): lax.all_gather(stored_memory_locator, 'cache', axis=0, tiled=True)  22.4 us
    all_to_all x1, waiting for transfers between devices, body(): lax.all_to_all(outgoing, 'cache', split_axis=2, concat_axis=0, tiled=True)  10.7 us
    transpose x4, local copies, waits for them, and re-layouts, arrange(): values.reshape(blocks, GROUP, head_count, group_features)  9.08 us
    dot_general x2, matrix products, advance(): scores = jnp.einsum('htc,hjc->htj', queries, scaled_keys, precision=highest)  8.41 us
    mul x2, other arithmetic, advance(): scaled_keys = address_portion * jnp.exp(-decay_sum)  6.86 us
    dot_general x2, matrix products, advance(): jnp.einsum('hjc,hjv->hcv', carried, value_part, precision=highest)  6.49 us
    all_to_all x1, starting transfers between devices, body(): lax.all_to_all(selected, 'cache', split_axis=0, concat_axis=0, tiled=True)  3.83 us
    dot_general x2, matrix products, advance(): jnp.einsum('htc,hcv->htv', queries, carry_state, precision=highest)  3.55 us
  transfers between devices with their start and end apart: 2, of which 1 were waited for; matrix products, arithmetic and copies ran while one was open for 10% of the time, Pallas kernels for 0%

commit v1 on v0

v1 whole, which is shorter than its diff:
```python
import functools

import jax
import jax.numpy as jnp
from jax import lax
from jax.experimental import pallas as pl
from jax.experimental.pallas import tpu as pltpu
from jax.sharding import PartitionSpec as P

GROUP = 64
HITS = 2
F32 = jnp.float32
BF16 = jnp.bfloat16


def split(x):
    hi = x.astype(BF16)
    lo = (x - hi.astype(F32)).astype(BF16)
    return hi, lo


def mm(a, b):
    return lax.dot_general(a, b, (((1,), (0,)), ((), ())), preferred_element_type=F32)


def mm_nt(a, b):
    return lax.dot_general(a, b, (((1,), (1,)), ((), ())), preferred_element_type=F32)


def mm_tn(a, b):
    return lax.dot_general(a, b, (((0,), (0,)), ((), ())), preferred_element_type=F32)


def lane_of(rows, lanes):
    return lax.broadcasted_iota(jnp.int32, (rows, lanes), 1)


def diag_pair(x, first):
    zero = jnp.zeros_like(x)
    return jnp.concatenate([jnp.where(first, x, zero), jnp.where(first, zero, x)], axis=0)


def pack_kernel(table_ref, saved_ref, out_ref, held, packed, in_sem, out_sem, *, parts):
    devices = out_ref.shape[0]
    rows = out_ref.shape[2]
    slots, heads, chans, _ = saved_ref.shape
    me = lax.axis_index("cache")

    def scan(i, used):
        bit = lax.shift_left(jnp.int32(1), table_ref[i, 1])
        return used | jnp.where(table_ref[i, 0] == me, bit, 0)

    used = lax.fori_loop(0, devices, scan, jnp.int32(0), unroll=min(8, devices))
    first = jnp.int32(0)
    second = jnp.int32(0)
    for s in reversed(range(slots)):
        has = (lax.shift_right_logical(used, s) & 1) == 1
        second = jnp.where(has, first, second)
        first = jnp.where(has, s, first)
    chosen = (first, second)
    step = heads // parts

    def load(part, hit):
        return pltpu.make_async_copy(
            saved_ref.at[chosen[hit], pl.ds(part * step, step)],
            held.at[hit, pl.ds(part * step, step)],
            in_sem.at[part, hit],
        )

    span = devices // parts

    def store(part, hit):
        return pltpu.make_async_copy(
            packed.at[pl.ds(part * span, span), hit],
            out_ref.at[pl.ds(part * span, span), hit],
            out_sem.at[part, hit],
        )

    for part in range(parts):
        for hit in range(HITS):
            load(part, hit).start()
    for part in range(parts):
        for hit in range(HITS):
            load(part, hit).wait()
            even = held[hit, pl.ds(part * step, step // 2, 2)]
            odd = held[hit, pl.ds(part * step + 1, step // 2, 2)]
            both = jnp.concatenate([even, odd], axis=-1)
            packed[part * span : (part + 1) * span, hit] = both.reshape(span, rows, 2 * chans)
            store(part, hit).start()
    for part in range(parts):
        for hit in range(HITS):
            store(part, hit).wait()


def pick_kernel(wanted_ref, arrived_ref, out_ref, held, in_sem, out_sem):
    devices = out_ref.shape[0]

    def load(d):
        w = wanted_ref[d]
        return pltpu.make_async_copy(
            arrived_ref.at[w // HITS, w % HITS], held.at[d], in_sem.at[d]
        )

    def store(d):
        return pltpu.make_async_copy(held.at[d], out_ref.at[d], out_sem.at[d])

    def each(f):
        lax.fori_loop(0, devices, lambda d, c: (f(d), c)[1], 0, unroll=min(8, devices))

    def turn(d):
        load(d).wait()
        store(d).start()

    each(lambda d: load(d).start())
    each(turn)
    each(lambda d: store(d).wait())


def inner_kernel(r_ref, k_ref, v_ref, f_ref, u_ref, o_ref, q_ref, part_ref, dec_ref):
    length, lanes = r_ref.shape
    wide = 2 * GROUP
    first = lane_of(GROUP, wide) < GROUP
    position = lane_of(GROUP, wide) % GROUP
    token = lax.broadcasted_iota(jnp.int32, (GROUP, wide), 0)
    lower = token > position
    row = lax.broadcasted_iota(jnp.int32, (length, length), 0)
    col = lax.broadcasted_iota(jnp.int32, (length, length), 1)
    triangle = ((row >= col) & (row // GROUP == col // GROUP)).astype(F32).astype(BF16)
    w_row = lax.broadcasted_iota(jnp.int32, (wide, wide), 0)
    w_col = lax.broadcasted_iota(jnp.int32, (wide, wide), 1)
    head_ones = (w_row // GROUP == w_col // GROUP).astype(F32).astype(BF16)
    ones = jnp.ones((length, wide), BF16)
    chunks = length // GROUP

    for pair in range(lanes // wide):
        at = slice(pair * wide, (pair + 1) * wide)
        f = f_ref[:, at]
        r = r_ref[:, at].astype(F32)
        k = k_ref[:, at].astype(F32)
        v = v_ref[:, at]
        cum = mm(triangle, f)
        q = r * jnp.exp(f.astype(F32) - cum)
        ks = k * jnp.exp(cum)
        x_hi, x_lo = split(r * u_ref[:, at] * k)
        bonus = mm(x_hi, head_ones) + mm(x_lo, head_ones)
        total = mm_tn(f, ones)
        dec_ref[pair] = jnp.exp(-jnp.where(first, total[:GROUP], total[GROUP:]))
        decays = [jnp.exp(-cum[(c + 1) * GROUP - 1 : (c + 1) * GROUP]) for c in range(chunks)]
        state = None
        start = None
        weights = []
        for c in range(chunks):
            rows = slice(c * GROUP, (c + 1) * GROUP)
            q_c = q[rows]
            q_hi, q_lo = split(q_c)
            k_hi, k_lo = split(ks[rows])
            v_c = v[rows]
            kd_hi = diag_pair(k_hi, first)
            kd_lo = diag_pair(k_lo, first)
            scores = mm_nt(q_hi, kd_hi) + mm_nt(q_lo, kd_hi) + mm_nt(q_hi, kd_lo)
            s_hi, s_lo = split(jnp.where(lower, scores, 0.0))
            vd = diag_pair(v_c, first)
            out = bonus[rows] * v_c.astype(F32) + mm(s_hi, vd) + mm(s_lo, vd)
            if c:
                p_hi, p_lo = split(state)
                pd_hi = diag_pair(p_hi, first)
                pd_lo = diag_pair(p_lo, first)
                out = out + mm(q_hi, pd_hi) + mm(q_lo, pd_hi) + mm(q_hi, pd_lo)
                q_c = q_c * start
                q_hi, q_lo = split(q_c)
            o_ref[rows, at] = out
            q_ref[rows, 2 * pair * wide : (2 * pair + 1) * wide] = q_hi
            q_ref[rows, (2 * pair + 1) * wide : (2 * pair + 2) * wide] = q_lo
            carried = ks[rows] * decays[c]
            if c < chunks - 1:
                c_hi, c_lo = split(carried)
                full = mm_tn(c_hi, v_c) + mm_tn(c_lo, v_c)
                grown = jnp.where(first, full[:GROUP], full[GROUP:])
                if state is not None:
                    total_c = mm_tn(f[rows], ones[rows])
                    keep = jnp.exp(-jnp.where(first, total_c[:GROUP], total_c[GROUP:]))
                    grown = grown + keep * state
                state = grown
                start = decays[c] if start is None else start * decays[c]
            for later in range(c + 1, chunks):
                carried = carried * decays[later]
            weights.append(carried)
        c_hi, c_lo = split(jnp.concatenate(weights, axis=0))
        full = mm_tn(c_hi, v) + mm_tn(c_lo, v)
        part_ref[pair] = jnp.where(first, full[:GROUP], full[GROUP:])


def outer_kernel(s_ref, o_ref, q_ref, part_ref, dec_ref, g_ref, gain_ref, bias_ref, mixed_ref, final_ref):
    length, lanes = o_ref.shape
    wide = 2 * GROUP
    first = lane_of(GROUP, wide) < GROUP
    w_row = lax.broadcasted_iota(jnp.int32, (wide, wide), 0)
    w_col = lax.broadcasted_iota(jnp.int32, (wide, wide), 1)
    mean_w = jnp.where(w_row // GROUP == w_col // GROUP, 1.0 / GROUP, 0.0).astype(BF16)
    for pair in range(lanes // wide):
        at = slice(pair * wide, (pair + 1) * wide)
        s = s_ref[pair]
        sd = diag_pair(s, first)
        q_hi = q_ref[:, 2 * pair * wide : (2 * pair + 1) * wide]
        q_lo = q_ref[:, (2 * pair + 1) * wide : (2 * pair + 2) * wide]
        out = o_ref[:, at] + mm(q_hi, sd) + mm(q_lo, sd)
        hi, lo = split(out)
        centered = out - (mm(hi, mean_w) + mm(lo, mean_w))
        hi, lo = split(centered * centered)
        var = mm(hi, mean_w) + mm(lo, mean_w)
        normed = centered * lax.rsqrt(var + 1e-05)
        g = g_ref[:, at].astype(F32)
        gate = g / (1.0 + jnp.exp(-g))
        mixed_ref[:, at] = ((normed * gain_ref[:, at] + bias_ref[:, at]) * gate).astype(BF16)
        last = dec_ref[pair] * s.astype(F32) + part_ref[pair]
        final_ref[2 * pair] = last[:, :GROUP]
        final_ref[2 * pair + 1] = last[:, GROUP:]


def body(
    reception_vectors,
    address_vectors,
    payload_vectors,
    emission_switch_preact,
    fading_rates,
    present_extra_coefficient,
    saved_memory_matrix,
    layernorm_scale,
    layernorm_shift,
    stored_memory_locator,
):
    devices = lax.axis_size("cache")
    heads, chans = present_extra_coefficient.shape
    slots = saved_memory_matrix.shape[0]
    length, lanes = reception_vectors.shape[1:]
    pairs = heads // 2
    wide = 2 * chans
    rows = pairs * chans // devices
    parts = min(4, devices)

    table = lax.all_to_all(
        jnp.broadcast_to(stored_memory_locator, (devices, 2)), "cache", 0, 0, tiled=True
    )

    anywhere = pl.BlockSpec(memory_space=pl.ANY)
    scalars = pl.BlockSpec(memory_space=pltpu.SMEM)
    outgoing = pl.pallas_call(
        functools.partial(pack_kernel, parts=parts),
        name="pack",
        out_shape=jax.ShapeDtypeStruct((devices, HITS, rows, wide), BF16),
        in_specs=[scalars, anywhere],
        out_specs=anywhere,
        scratch_shapes=[
            pltpu.VMEM((HITS, heads, chans, chans), BF16),
            pltpu.VMEM((devices, HITS, rows, wide), BF16),
            pltpu.SemaphoreType.DMA((parts, HITS)),
            pltpu.SemaphoreType.DMA((parts, HITS)),
        ],
        cost_estimate=pl.CostEstimate(flops=0, transcendentals=0, bytes_accessed=3 << 20),
    )(table, saved_memory_matrix)
    arrived = lax.all_to_all(outgoing, "cache", 0, 0, tiled=True)

    owner = table[:, 0]
    slot = table[:, 1]
    same = owner[:, None] == owner[None, :]
    ids = jnp.arange(slots, dtype=jnp.int32)
    named = jnp.any(same[:, :, None] & (slot[None, :, None] == ids), axis=1)
    rank = jnp.sum((named & (ids[None, :] < slot[:, None])).astype(jnp.int32), axis=1)
    wanted = owner * HITS + rank

    steps = 4
    block = lanes // steps
    per = pairs // steps
    tokens = pl.BlockSpec((length, block), lambda i: (0, i))
    row_of = pl.BlockSpec((1, block), lambda i: (0, i))
    states = pl.BlockSpec((per, chans, wide), lambda i: (i, 0, 0))
    doubled = pl.BlockSpec((length, 2 * block), lambda i: (0, i))
    inner, queries, partial, decay = pl.pallas_call(
        inner_kernel,
        name="inner",
        grid=(steps,),
        out_shape=(
            jax.ShapeDtypeStruct((length, lanes), F32),
            jax.ShapeDtypeStruct((length, 2 * lanes), BF16),
            jax.ShapeDtypeStruct((pairs, chans, wide), F32),
            jax.ShapeDtypeStruct((pairs, chans, wide), F32),
        ),
        in_specs=[tokens, tokens, tokens, tokens, row_of],
        out_specs=(tokens, doubled, states, states),
        cost_estimate=pl.CostEstimate(flops=1 << 32, transcendentals=1 << 20, bytes_accessed=16 << 20),
    )(
        reception_vectors[0],
        address_vectors[0],
        payload_vectors[0],
        fading_rates[0],
        present_extra_coefficient.reshape(1, lanes),
    )

    selected = pl.pallas_call(
        pick_kernel,
        name="pick",
        out_shape=jax.ShapeDtypeStruct((devices, rows, wide), BF16),
        in_specs=[scalars, anywhere],
        out_specs=anywhere,
        scratch_shapes=[
            pltpu.VMEM((devices, rows, wide), BF16),
            pltpu.SemaphoreType.DMA((devices,)),
            pltpu.SemaphoreType.DMA((devices,)),
        ],
        cost_estimate=pl.CostEstimate(flops=0, transcendentals=0, bytes_accessed=1 << 20),
    )(wanted, arrived)
    delivered = lax.all_to_all(selected, "cache", 0, 0, tiled=True)

    mixed, final = pl.pallas_call(
        outer_kernel,
        name="outer",
        grid=(steps,),
        out_shape=(
            jax.ShapeDtypeStruct((length, lanes), BF16),
            jax.ShapeDtypeStruct((heads, chans, chans), F32),
        ),
        in_specs=[states, tokens, doubled, states, states, tokens, row_of, row_of],
        out_specs=(tokens, pl.BlockSpec((2 * per, chans, chans), lambda i: (i, 0, 0))),
        cost_estimate=pl.CostEstimate(flops=1 << 30, transcendentals=1 << 20, bytes_accessed=8 << 20),
    )(
        delivered.reshape(pairs, chans, wide),
        inner,
        queries,
        partial,
        decay,
        emission_switch_preact[0],
        layernorm_scale.reshape(1, lanes),
        layernorm_shift.reshape(1, lanes),
    )
    return (mixed[None], final[None])


def solution(mesh):
    in_specs = (
        P(("rep", "cache"), None, "head"),
        P(("rep", "cache"), None, "head"),
        P(("rep", "cache"), None, "head"),
        P(("rep", "cache"), None, "head"),
        P(("rep", "cache"), None, "head"),
        P("head", None),
        P(("rep", "cache"), "head", None, None),
        P("head"),
        P("head"),
        P(("rep", "cache"), None),
    )
    out_specs = (P(("rep", "cache"), None, "head"), P(("rep", "cache"), "head", None, None))
    return jax.shard_map(body, mesh=mesh, in_specs=in_specs, out_specs=out_specs, check_vma=False)
```

time: 108 us -> 64.1 us (0.59)
  Pallas kernels: 0 us -> 25.3 us
  matrix products: 23.9 us -> 0 us
  local copies, waits for them, and re-layouts: 24.6 us -> 3.59 us
  other arithmetic: 17.1 us -> 0.78 us
  blocking collectives: 22.4 us -> 13.6 us
  waiting for transfers between devices: 10.7 us -> 12.5 us
    pallas_call x0 -> x4, Pallas kernels: none -> 25.3 us  [the longest x1 13.5 us: body(): pl.pallas_call(inner_kernel, name='inner', grid=(steps,), out_shape=(jax....]
    dot_general x11 -> x0, matrix products: 23.9 us -> none  [the longest x2 8.41 us: advance(): scores = jnp.einsum('htc,hjc->htj', queries, scaled_keys, precision=highest)]
    all_gather x1 -> x0, blocking collectives: 22.4 us -> none  [body(): lax.all_gather(stored_memory_locator, 'cache', axis=0, tiled=True)]
    all_to_all x0 -> x1, blocking collectives: none -> 13.6 us  [body(): lax.all_to_all(jnp.broadcast_to(stored_memory_locator, (devices, 2)), 'ca...]
    transpose x5 -> x0, local copies, waits for them, and re-layouts: 11.4 us -> none  [the longest x4 9.08 us: arrange(): values.reshape(blocks, GROUP, head_count, group_features)]
    mul x2 -> x0, other arithmetic: 6.86 us -> none  [advance(): scaled_keys = address_portion * jnp.exp(-decay_sum)]
    reshape x3 -> x1, local copies, waits for them, and re-layouts: 5.78 us -> 0.68 us  [body(): present_extra_coefficient.reshape(1, lanes)]
    reduce_sum x3 -> x1, other arithmetic: 4.08 us -> 0.02 us  [body(): jnp.sum((named & (ids[None, :] < slot[:, None])).astype(jnp.int32), axis=1)]
  transfers between devices with their start and end apart: 2 -> 2, of which waited for: 1 -> 1; matrix products, arithmetic and copies ran while one was open for 10% -> 2% of each run, Pallas kernels for 0% -> 21%
where the time goes in v1:
time: 64.1 us; the launch traced here: 63.5 us
  Pallas kernels  25.3 us (39%)
  blocking collectives  13.6 us (21%)
  waiting for transfers between devices  12.5 us (20%)
  starting transfers between devices  7.18 us (11%)
  local copies, waits for them, and re-layouts  3.59 us (6%)
  other arithmetic  0.78 us (1%)
  between operations  0.7 us (1%)
    all_to_all x1, blocking collectives, body(): lax.all_to_all(jnp.broadcast_to(stored_memory_locator, (devices, 2)), 'ca...  13.6 us
    pallas_call x1, Pallas kernels, body(): pl.pallas_call(inner_kernel, name='inner', grid=(steps,), out_shape=(jax....  13.5 us
    all_to_all x1, waiting for transfers between devices, body(): arrived = lax.all_to_all(outgoing, 'cache', 0, 0, tiled=True)  12.4 us
    pallas_call x1, Pallas kernels, body(): pl.pallas_call(outer_kernel, name='outer', grid=(steps,), out_shape=(jax....  6.18 us
    all_to_all x1, starting transfers between devices, body(): delivered = lax.all_to_all(selected, 'cache', 0, 0, tiled=True)  3.67 us
    all_to_all x1, starting transfers between devices, body(): arrived = lax.all_to_all(outgoing, 'cache', 0, 0, tiled=True)  3.51 us
    pallas_call x1, Pallas kernels, body(): pl.pallas_call(functools.partial(pack_kernel, parts=parts), name='pack',...  3.25 us
    pallas_call x1, Pallas kernels, body(): pl.pallas_call(pick_kernel, name='pick', out_shape=jax.ShapeDtypeStruct((...  2.32 us
  transfers between devices with their start and end apart: 2, of which 1 were waited for; matrix products, arithmetic and copies ran while one was open for 2% of the time, Pallas kernels for 21%

profile of v1, /device:TPU:0, one launch (start us, length us, event | category | flops | bytes accessed | tf_op | source)
XLA Modules:
  0.0 63.5 jit_solution(14305310749787335428)
XLA Ops:
  0.6 0.7 %broadcast_in_dim.6 = s32[8,1,2]{2,1,0:T(1,128)S(1)} broadcast(s32[2]{0:T(128)} %bitcast.22), dimensions={2} | broadcast | bytes 72 | tf_op jit(solution)/shard_map/broadcast_in_dim | solution.py:242
  1.3 13.6 %all_to_all.18 = s32[8,1,2]{2,1,0:T(1,128)S(1)} all-to-all(s32[8,1,2]{2,1,0:T(1,128)S(1)} %broadcast_in_dim.6), channel_id=1, replica_groups=mesh['rep'=2,'cache'=8,'head'=2] {'cache'}, dimensions={0} | all-to-all | bytes 128 | tf_op jit(solution)/shard_map/all_to_all | solution.py:241
  14.8 0.1 copy.15
  14.9 0.7 %copy.16.table_ref = s32[8,2]{1,0:T(8,128)} copy(s32[8,2]{0,1:T(2,128)S(1)} %bitcast.19) | data formatting | bytes 128 | tf_op jit(solution)/shard_map/all_to_all | solution.py:241
  15.6 0.0 copy-start.2
  15.6 3.2 %pack.1 = bf16[8,2,128,128]{3,2,1,0:T(8,128)(2,1)} custom-call(s32[8,2]{1,0:T(8,128)} %copy.16.table_ref, bf16[4,32,64,64]{3,2,1,0:T(8,128)(2,1)} %saved_ref.1), custom_call_target="tpu_custom_call" | custom-call | bytes 3145728 | tf_op jit(solution)/shard_map/pack/pallas_call | solution.py:247
  18.9 3.5 %all-to-all-start.1 = ((bf16[8,2,128,128]{3,2,1,0:T(8,128)(2,1)}), bf16[8,2,128,128]{3,2,1,0:T(8,128)(2,1)S(1)}, u32[]{:S(2)}, u32[]{:S(2)}) async-start(bf16[8,2,128,128]{3,2,1,0:T(8,128)(2,1)} %pack.1), calls=%async_computation.1 | async-start | bytes 1048576 | tf_op jit(solution)/shard_map/all_to_all | solution.py:261
  22.4 0.1 broadcast_compare_fusion
  22.5 0.2 and_reduce_fusion
  22.7 0.5 multiply_add_fusion.wanted_ref
  23.2 12.4 %all-to-all-done.1.arrived_ref = bf16[8,2,128,128]{3,2,1,0:T(8,128)(2,1)S(1)} async-done(((bf16[8,2,128,128]{3,2,1,0:T(8,128)(2,1)}), bf16[8,2,128,128]{3,2,1,0:T(8,128)(2,1)S(1)}, u32[]{:S(2)}, u32[]{:S(2)}) %all-to-all-start.1) | async-done | bytes 524320 | tf_op jit(solution)/shard_map/all_to_all | solution.py:261
  35.6 0.0 copy-start
  35.6 0.8 %copy-done = bf16[8,2,128,128]{3,2,1,0:T(8,128)(2,1)} copy-done((bf16[8,2,128,128]{3,2,1,0:T(8,128)(2,1)}, bf16[8,2,128,128]{3,2,1,0:T(8,128)(2,1)S(1)}, u32[]{:S(2)}) %copy-start) | copy-done | bytes 524312
  36.4 2.3 %pick.1 = bf16[8,128,128]{2,1,0:T(8,128)(2,1)} custom-call(s32[8]{0:T(128)} %multiply_add_fusion.wanted_ref, bf16[8,2,128,128]{3,2,1,0:T(8,128)(2,1)} %copy-done), custom_call_target="tpu_custom_call" | custom-call | bytes 1048576 | tf_op jit(solution)/shard_map/pick/pallas_call | solution.py:299
  38.7 3.7 %all-to-all-start.2 = ((bf16[8,128,128]{2,1,0:T(8,128)(2,1)}), bf16[8,128,128]{2,1,0:T(8,128)(2,1)S(1)}, u32[]{:S(2)}, u32[]{:S(2)}) async-start(bf16[8,128,128]{2,1,0:T(8,128)(2,1)} %pick.1), calls=%async_computation.2 | async-start | bytes 524288 | tf_op jit(solution)/shard_map/all_to_all | solution.py:312
  42.4 0.0 copy-done.2
  42.4 0.7 %reshape.78.u_ref = f32[1,2048]{1,0:T(1,128)} reshape(f32[32,64]{1,0:T(8,128)S(1)} %copy-done.2) | data formatting | bytes 16384 | tf_op jit(solution)/shard_map/reshape | solution.py:296
  43.1 13.5 %inner.1 = (f32[128,2048]{1,0:T(8,128)}, bf16[128,4096]{1,0:T(8,128)(2,1)}, f32[16,64,128]{2,1,0:T(8,128)}, f32[16,64,128]{2,1,0:T(8,128)}) custom-call(bf16[128,2048]{1,0:T(8,128)(2,1)} %bitcast.23, bf16[128,2048]{1,0:T(8,128)(2,1)} %bitcast.24, bf16[128,2048]{1,0:T(8,128)(2,1)} %bitcast.25, bf16[128,2048]{1,0:T(8,128)(2,1)} %bitcast.26, ...), custom_call_target="tpu_custom_call" | custom-call | flops 4294967296 | bytes 16777216 | tf_op jit(solution)/shard_map/inner/pallas_call | solution.py:278
  56.6 0.0 all-to-all-done.2
  56.6 0.0 copy-start.1
  56.6 0.7 %copy-done.1 = bf16[8,128,128]{2,1,0:T(8,128)(2,1)} copy-done((bf16[8,128,128]{2,1,0:T(8,128)(2,1)}, bf16[8,128,128]{2,1,0:T(8,128)(2,1)S(1)}, u32[]{:S(2)}) %copy-start.1) | copy-done | bytes 262168
  57.3 6.2 %outer.1 = (bf16[128,2048]{1,0:T(8,128)(2,1)}, f32[32,64,64]{2,1,0:T(8,128)}) custom-call(bf16[16,64,128]{2,1,0:T(8,128)(2,1)} %bitcast.18, f32[128,2048]{1,0:T(8,128)} %get-tuple-element.8.o_ref, bf16[128,4096]{1,0:T(8,128)(2,1)} %get-tuple-element.9.q_ref, f32[16,64,128]{2,1,0:T(8,128)} %get-tuple-element.10.part_ref, ...), custom_call_target="tpu_custom_call" | custom-call | flops 1073741824 | bytes 8388608 | tf_op jit(solution)/shard_map/outer/pallas_call | solution.py:314
  (3 shorter events, 0.0 us)
Async XLA Ops:
  15.6 26.8 %copy-start.2 = (f32[32,64]{1,0:T(8,128)S(1)}, f32[32,64]{1,0:T(8,128)}, u32[]{:S(2)}) copy-start(f32[32,64]{1,0:T(8,128)} %param.15) | copy-start | bytes 24580
  18.9 16.8 %all-to-all-start.1 = ((bf16[8,2,128,128]{3,2,1,0:T(8,128)(2,1)}), bf16[8,2,128,128]{3,2,1,0:T(8,128)(2,1)S(1)}, u32[]{:S(2)}, u32[]{:S(2)}) async-start(bf16[8,2,128,128]{3,2,1,0:T(8,128)(2,1)} %pack.1), calls=%async_computation.1 | async-start | bytes 1048576 | tf_op jit(solution)/shard_map/all_to_all | solution.py:261
  35.6 0.8 %copy-start = (bf16[8,2,128,128]{3,2,1,0:T(8,128)(2,1)}, bf16[8,2,128,128]{3,2,1,0:T(8,128)(2,1)S(1)}, u32[]{:S(2)}) copy-start(bf16[8,2,128,128]{3,2,1,0:T(8,128)(2,1)S(1)} %all-to-all-done.1.arrived_ref) | copy-start | bytes 1572868
  38.7 17.9 %all-to-all-start.2 = ((bf16[8,128,128]{2,1,0:T(8,128)(2,1)}), bf16[8,128,128]{2,1,0:T(8,128)(2,1)S(1)}, u32[]{:S(2)}, u32[]{:S(2)}) async-start(bf16[8,128,128]{2,1,0:T(8,128)(2,1)} %pick.1), calls=%async_computation.2 | async-start | bytes 524288 | tf_op jit(solution)/shard_map/all_to_all | solution.py:312
  56.6 0.7 %copy-start.1 = (bf16[8,128,128]{2,1,0:T(8,128)(2,1)}, bf16[8,128,128]{2,1,0:T(8,128)(2,1)S(1)}, u32[]{:S(2)}) copy-start(bf16[8,128,128]{2,1,0:T(8,128)(2,1)S(1)} %all-to-all-done.2) | copy-start | bytes 786436
